TPU v7x, 32 devices: a whole 2x2x4 slice. The times are simulated.
32 devices in a mesh: dp: 4 (over x, core), blk: 8 (over z, y).
Axes of the slice: x: 2, y: 2, z: 4, core: 2. Of those that a mesh axis runs over, the one named last changes fastest.
Arguments:
- hidden_in: bfloat16 [2048, 8, 1024], P('blk', 'dp'), may hold values from -6 to 6
- first_values: bfloat16 [2048, 8, 1024], P('blk', 'dp'), may hold values from -13 to 13
- doc_lengths: int32 [8, 8], P('dp'), may hold values from 1 to 1024, 2048 in all within a row
- w_query: bfloat16 [1024, 1024], replicated, may hold values from -0.25 to 0.25
- w_key: bfloat16 [1024, 1024], replicated, may hold values from -0.25 to 0.25
- w_value: bfloat16 [1024, 1024], replicated, may hold values from -0.1875 to 0.1875
- w_out: bfloat16 [1024, 1024], replicated, may hold values from -0.75 to 0.75
- w_gate: bfloat16 [1024, 2816], replicated, may hold values from -0.1875 to 0.1875
- w_up: bfloat16 [1024, 2816], replicated, may hold values from -0.1875 to 0.1875
- w_down: bfloat16 [2816, 1024], replicated, may hold values from -0.109375 to 0.109375
- attn_gain: float32 [1024], replicated, may hold values from 0.5 to 1.5
- ffn_gain: float32 [1024], replicated, may hold values from 0.5 to 1.5
- out_cotangent: bfloat16 [2048, 8, 1024], P('blk', 'dp'), may hold values from -6 to 6
Outputs:
- block_out: bfloat16 [2048, 8, 1024], P('blk', 'dp')
- grad_input: float32 [2048, 8, 1024], P('blk', 'dp')
- grad_first: float32 [2048, 8, 1024], P('blk', 'dp')
- grad_query: float32 [1024, 1024], P('dp', 'blk')
- grad_key: float32 [1024, 1024], P('dp', 'blk')
- grad_value: float32 [1024, 1024], P('dp', 'blk')
- grad_project: float32 [1024, 1024], P('dp', 'blk')
- grad_gate: float32 [1024, 2816], P('dp', 'blk')
- grad_up: float32 [1024, 2816], P('dp', 'blk')
- grad_down: float32 [2816, 1024], P('dp', 'blk')
- grad_attn_gain: float32 [1024], replicated
- grad_ffn_gain: float32 [1024], replicated
- first_msq: float32 [], replicated
- mixed_msq: float32 [], replicated
Inputs may be any that keep to these rules, and one draw needn't show every extreme that they name: `doc_lengths`: the 8 lengths of a row sum to 2048.
All inputs are finite; a program needn't handle non-finite values.
Results may differ from a plain program's by a relative error of at most 0.033.
Values may be sent and summed in bfloat16 or wider, within the bound.
A program may use at most 320 MiB of HBM per device.

v0:
```python
import jax
import jax.numpy as jnp
from jax import lax
from jax.sharding import PartitionSpec as P

HEADS = 16
HEAD_DIM = 64
epsilon = 1e-06


def documents(doc_lengths, row_length):
    doc_ends = jnp.cumsum(doc_lengths, axis=1)
    places = jnp.arange(row_length, dtype=jnp.int32)
    passed = (doc_ends[:, None, :] <= places[None, :, None]).astype(jnp.int32)
    segment = jnp.sum(passed, axis=2)
    doc_start = jnp.sum(passed * doc_lengths[:, None, :], axis=2)
    return (segment, places[None, :] - doc_start)


def project(acts, weight):
    flat = acts.reshape(-1, acts.shape[-1])
    result = jnp.dot(flat, weight, preferred_element_type=jnp.float32)
    return result.reshape(acts.shape[:-1] + (weight.shape[1],))


def project_back(grads_in, weight):
    flat = grads_in.reshape(-1, grads_in.shape[-1])
    result = lax.dot_general(
        flat, weight, (((1,), (1,)), ((), ())), preferred_element_type=jnp.float32
    )
    return result.reshape(grads_in.shape[:-1] + (weight.shape[0],))


def weight_grad(acts, grads_in):
    flat_acts = acts.reshape(-1, acts.shape[-1])
    flat_grads = grads_in.reshape(-1, grads_in.shape[-1])
    return lax.dot_general(
        flat_acts, flat_grads, (((0,), (0,)), ((), ())), preferred_element_type=jnp.float32
    )


def rms_parts(values):
    inverse_rms = lax.rsqrt(jnp.mean(values * values, axis=-1, keepdims=True) + epsilon)
    return (values * inverse_rms, inverse_rms)


def norm_back(d_normed, normed, inverse_rms):
    return inverse_rms * (d_normed - normed * jnp.mean(d_normed * normed, axis=-1, keepdims=True))


def rope_tables(positions):
    half_dim = HEAD_DIM // 2
    inverse_freq = jnp.power(10000.0, -jnp.arange(half_dim, dtype=jnp.float32) * 2.0 / HEAD_DIM)
    angles = jnp.transpose(positions).astype(jnp.float32)[:, :, None] * inverse_freq[None, None, :]
    return (jnp.cos(angles)[:, :, None, :], jnp.sin(angles)[:, :, None, :])


def rotate(values, cos_table, sin_table):
    half_dim = HEAD_DIM // 2
    shaped = values.reshape(values.shape[:-1] + (HEADS, HEAD_DIM))
    first_half = shaped[..., :half_dim]
    second_half = shaped[..., half_dim:]
    turned = jnp.concatenate(
        [
            first_half * cos_table - second_half * sin_table,
            second_half * cos_table + first_half * sin_table,
        ],
        axis=-1,
    )
    return turned.reshape(values.shape)


def body(
    hidden_in,
    first_values,
    doc_lengths,
    w_query,
    w_key,
    w_value,
    w_out,
    w_gate,
    w_up,
    w_down,
    attn_gain,
    ffn_gain,
    out_cotangent,
):
    local_len, seq_count, model_width = hidden_in.shape
    cycle_size = lax.axis_size("blk")
    row_length = local_len * cycle_size
    offset = lax.axis_index("blk") * local_len
    score_scale = HEAD_DIM ** (-0.5)
    segment_all, position_all = documents(doc_lengths, row_length)
    segment_own = lax.dynamic_slice_in_dim(segment_all, offset, local_len, 1)
    position_own = lax.dynamic_slice_in_dim(position_all, offset, local_len, 1)
    query_index = offset + jnp.arange(local_len, dtype=jnp.int32)
    cos_table, sin_table = rope_tables(position_own)
    resid_in = hidden_in.astype(jnp.float32)
    normed_one, inv_one = rms_parts(resid_in)
    normed_in = (normed_one * attn_gain).astype(jnp.bfloat16)
    queries = rotate(project(normed_in, w_query), cos_table, sin_table).astype(jnp.bfloat16)
    keys_rot = rotate(project(normed_in, w_key), cos_table, sin_table).astype(jnp.bfloat16)
    first_f = first_values.astype(jnp.float32)
    mixed = 0.5 * project(normed_in, w_value) + 0.5 * first_f
    mixed_low = mixed.astype(jnp.bfloat16)
    first_sq = jnp.sum(first_f * first_f)
    mixed_sq = jnp.sum(mixed * mixed)
    query_four = queries.reshape(local_len, seq_count, HEADS, HEAD_DIM)

    def allowed_pairs(start, n_keys):
        key_index = start + jnp.arange(n_keys, dtype=jnp.int32)
        segment_key = lax.dynamic_slice_in_dim(segment_all, start, n_keys, 1)
        allowed = (key_index[None, None, :] <= query_index[None, :, None]) & (
            segment_key[:, None, :] == segment_own[:, :, None]
        )
        return allowed[:, None]

    def piece_step(running, key_piece, value_piece, start):
        run_max, run_sum, run_acc = running
        n_keys = key_piece.shape[0]
        allowed = allowed_pairs(start, n_keys)
        key_four = key_piece.reshape(n_keys, seq_count, HEADS, HEAD_DIM)
        value_four = value_piece.reshape(n_keys, seq_count, HEADS, HEAD_DIM)
        scores = (
            jnp.einsum("qshd,kshd->shqk", query_four, key_four, preferred_element_type=jnp.float32)
            * score_scale
        )
        new_max = jnp.maximum(run_max, jnp.max(jnp.where(allowed, scores, -1e30), axis=-1))
        weights = jnp.where(allowed, jnp.exp(scores - new_max[..., None]), 0.0)
        factor = jnp.exp(run_max - new_max)
        run_sum = run_sum * factor + jnp.sum(weights, axis=-1)
        run_acc = run_acc * factor[..., None] + jnp.einsum(
            "shqk,kshd->shqd",
            weights.astype(jnp.bfloat16),
            value_four,
            preferred_element_type=jnp.float32,
        )
        return (new_max, run_sum, run_acc)

    start_state = (
        jnp.full((seq_count, HEADS, local_len), -1e30, jnp.float32),
        jnp.zeros((seq_count, HEADS, local_len), jnp.float32),
        jnp.zeros((seq_count, HEADS, local_len, HEAD_DIM), jnp.float32),
    )
    running = start_state
    key_piece = lax.all_gather(keys_rot, "blk", axis=0, tiled=True)
    value_piece = lax.all_gather(mixed_low, "blk", axis=0, tiled=True)
    n_keys = key_piece.shape[0]
    step_rows = min(512, n_keys)
    n_steps = n_keys // step_rows

    def inner_step(fold_state, block_item):
        return (piece_step(fold_state, block_item[0], block_item[1], block_item[2]), None)

    starts = jnp.arange(n_steps, dtype=jnp.int32) * step_rows
    running, unused = lax.scan(
        inner_step,
        running,
        (
            key_piece.reshape(n_steps, step_rows, seq_count, model_width),
            value_piece.reshape(n_steps, step_rows, seq_count, model_width),
            starts,
        ),
    )
    run_max, run_sum, run_acc = running
    attn_four = jnp.transpose(run_acc / run_sum[..., None], (2, 0, 1, 3))
    attn_f = attn_four.reshape(local_len, seq_count, model_width)
    log_total = run_max + jnp.log(run_sum)
    attn_low = attn_f.astype(jnp.bfloat16)
    resid_mid = resid_in + project(attn_low, w_out)
    normed_two, inv_two = rms_parts(resid_mid)
    normed_mid = (normed_two * ffn_gain).astype(jnp.bfloat16)
    gate_pre = project(normed_mid, w_gate)
    up_pre = project(normed_mid, w_up)
    gate_act = jax.nn.silu(gate_pre)
    inner_low = (gate_act * up_pre).astype(jnp.bfloat16)
    block_out = (resid_mid + project(inner_low, w_down)).astype(jnp.bfloat16)
    grad_down = weight_grad(inner_low, out_cotangent)
    d_inner = project_back(out_cotangent, w_down)
    sigmoid_gate = jax.nn.sigmoid(gate_pre)
    d_gate = (d_inner * up_pre * sigmoid_gate * (1.0 + gate_pre * (1.0 - sigmoid_gate))).astype(
        jnp.bfloat16
    )
    d_up = (d_inner * gate_act).astype(jnp.bfloat16)
    grad_gate = weight_grad(normed_mid, d_gate)
    grad_up = weight_grad(normed_mid, d_up)
    d_normed_mid = project_back(d_gate, w_gate) + project_back(d_up, w_up)
    gain_two_grad = jnp.sum((d_normed_mid * normed_two).reshape(-1, model_width), axis=0)
    d_resid_mid = out_cotangent.astype(jnp.float32) + norm_back(
        d_normed_mid * ffn_gain, normed_two, inv_two
    )
    d_branch = d_resid_mid.astype(jnp.bfloat16)
    grad_project = weight_grad(attn_low, d_branch)
    d_attn = project_back(d_branch, w_out).astype(jnp.bfloat16)
    d_attn_four = d_attn.reshape(local_len, seq_count, HEADS, HEAD_DIM)
    delta_rows = jnp.transpose(
        jnp.sum(d_attn_four.astype(jnp.float32) * attn_four, axis=-1), (1, 2, 0)
    )
    back_keys, back_values = (
        lax.all_gather(keys_rot, "blk", axis=0, tiled=True),
        lax.all_gather(mixed_low, "blk", axis=0, tiled=True),
    )
    block_rows = min(512, row_length)
    n_blocks = row_length // block_rows
    block_starts = jnp.arange(n_blocks, dtype=jnp.int32) * block_rows

    def block_scores(key_four, value_four, start):
        allowed = allowed_pairs(start, block_rows)
        scores = (
            jnp.einsum("qshd,kshd->shqk", query_four, key_four, preferred_element_type=jnp.float32)
            * score_scale
        )
        probs = jnp.where(allowed, jnp.exp(scores - log_total[..., None]), 0.0)
        d_probs = jnp.einsum(
            "qshd,kshd->shqk", d_attn_four, value_four, preferred_element_type=jnp.float32
        )
        d_scores = (probs * (d_probs - delta_rows[..., None])).astype(jnp.bfloat16)
        return (probs, d_scores)

    def back_step(d_query_acc, block_item):
        key_block, value_block, start = block_item
        key_four = key_block.reshape(block_rows, seq_count, HEADS, HEAD_DIM)
        value_four = value_block.reshape(block_rows, seq_count, HEADS, HEAD_DIM)
        probs, d_scores = block_scores(key_four, value_four, start)
        d_query_acc = (
            d_query_acc
            + jnp.einsum("shqk,kshd->qshd", d_scores, key_four, preferred_element_type=jnp.float32)
            * score_scale
        )
        d_keys = (
            jnp.einsum("shqk,qshd->kshd", d_scores, query_four, preferred_element_type=jnp.float32)
            * score_scale
        )
        d_vals = jnp.einsum(
            "shqk,qshd->kshd",
            probs.astype(jnp.bfloat16),
            d_attn_four,
            preferred_element_type=jnp.float32,
        )
        joined = jnp.concatenate(
            [
                d_keys.reshape(block_rows, seq_count, model_width),
                d_vals.reshape(block_rows, seq_count, model_width),
            ],
            axis=-1,
        )
        return (d_query_acc, joined)

    d_query_rot, terms = lax.scan(
        back_step,
        jnp.zeros((local_len, seq_count, HEADS, HEAD_DIM), jnp.float32),
        (
            back_keys.reshape(n_blocks, block_rows, seq_count, model_width),
            back_values.reshape(n_blocks, block_rows, seq_count, model_width),
            block_starts,
        ),
    )
    terms = terms.reshape(row_length, seq_count, 2 * model_width)
    kv_grad = lax.psum_scatter(
        terms.astype(jnp.bfloat16), "blk", scatter_dimension=0, tiled=True
    ).astype(jnp.float32)
    d_key_rot = kv_grad[..., :model_width]
    d_mixed = kv_grad[..., model_width:]
    d_query_low = rotate(
        d_query_rot.reshape(local_len, seq_count, model_width), cos_table, -sin_table
    ).astype(jnp.bfloat16)
    d_key_low = rotate(d_key_rot, cos_table, -sin_table).astype(jnp.bfloat16)
    d_value_low = (0.5 * d_mixed).astype(jnp.bfloat16)
    grad_first = 0.5 * d_mixed
    grad_query = weight_grad(normed_in, d_query_low)
    grad_key = weight_grad(normed_in, d_key_low)
    grad_value = weight_grad(normed_in, d_value_low)
    d_normed_in = (
        project_back(d_query_low, w_query)
        + project_back(d_key_low, w_key)
        + project_back(d_value_low, w_value)
    )
    gain_one_grad = jnp.sum((d_normed_in * normed_one).reshape(-1, model_width), axis=0)
    grad_input = d_resid_mid + norm_back(d_normed_in * attn_gain, normed_one, inv_one)
    weight_grads = (grad_query, grad_key, grad_value, grad_project, grad_gate, grad_up, grad_down)
    partial_grads = (
        lax.psum_scatter(
            weight_grads[0].astype(jnp.bfloat16), "dp", scatter_dimension=0, tiled=True
        ).astype(jnp.float32),
        lax.psum_scatter(
            weight_grads[1].astype(jnp.bfloat16), "dp", scatter_dimension=0, tiled=True
        ).astype(jnp.float32),
        lax.psum_scatter(
            weight_grads[2].astype(jnp.bfloat16), "dp", scatter_dimension=0, tiled=True
        ).astype(jnp.float32),
        lax.psum_scatter(
            weight_grads[3].astype(jnp.bfloat16), "dp", scatter_dimension=0, tiled=True
        ).astype(jnp.float32),
        lax.psum_scatter(
            weight_grads[4].astype(jnp.bfloat16), "dp", scatter_dimension=0, tiled=True
        ).astype(jnp.float32),
        lax.psum_scatter(
            weight_grads[5].astype(jnp.bfloat16), "dp", scatter_dimension=0, tiled=True
        ).astype(jnp.float32),
        lax.psum_scatter(
            weight_grads[6].astype(jnp.bfloat16), "dp", scatter_dimension=0, tiled=True
        ).astype(jnp.float32),
    )
    summed = (
        lax.psum_scatter(
            partial_grads[0].astype(jnp.bfloat16), "blk", scatter_dimension=1, tiled=True
        ).astype(jnp.float32),
        lax.psum_scatter(
            partial_grads[1].astype(jnp.bfloat16), "blk", scatter_dimension=1, tiled=True
        ).astype(jnp.float32),
        lax.psum_scatter(
            partial_grads[2].astype(jnp.bfloat16), "blk", scatter_dimension=1, tiled=True
        ).astype(jnp.float32),
        lax.psum_scatter(
            partial_grads[3].astype(jnp.bfloat16), "blk", scatter_dimension=1, tiled=True
        ).astype(jnp.float32),
        lax.psum_scatter(
            partial_grads[4].astype(jnp.bfloat16), "blk", scatter_dimension=1, tiled=True
        ).astype(jnp.float32),
        lax.psum_scatter(
            partial_grads[5].astype(jnp.bfloat16), "blk", scatter_dimension=1, tiled=True
        ).astype(jnp.float32),
        lax.psum_scatter(
            partial_grads[6].astype(jnp.bfloat16), "blk", scatter_dimension=1, tiled=True
        ).astype(jnp.float32),
    )
    totals = lax.psum((gain_one_grad, gain_two_grad, first_sq, mixed_sq), ("dp", "blk"))
    n_entries = row_length * seq_count * lax.axis_size("dp") * model_width
    return (
        block_out,
        grad_input,
        grad_first,
        summed[0],
        summed[1],
        summed[2],
        summed[3],
        summed[4],
        summed[5],
        summed[6],
        totals[0],
        totals[1],
        totals[2] / n_entries,
        totals[3] / n_entries,
    )


def solution(mesh):
    in_specs = (
        P("blk", "dp", None),
        P("blk", "dp", None),
        P("dp", None),
        P(),
        P(),
        P(),
        P(),
        P(),
        P(),
        P(),
        P(),
        P(),
        P("blk", "dp", None),
    )
    out_specs = (
        P("blk", "dp", None),
        P("blk", "dp", None),
        P("blk", "dp", None),
        P("dp", "blk"),
        P("dp", "blk"),
        P("dp", "blk"),
        P("dp", "blk"),
        P("dp", "blk"),
        P("dp", "blk"),
        P("dp", "blk"),
        P(),
        P(),
        P(),
        P(),
    )
    return jax.shard_map(body, mesh=mesh, in_specs=in_specs, out_specs=out_specs, check_vma=False)
```

profile of v0, /device:TPU:0, one launch (start us, length us, event | category | flops | bytes accessed | tf_op | source)
XLA Modules:
  0.0 1740.5 jit_solution(13050748668814698923)
XLA Ops:
  42.2 99.5 %all-gather.5.cloned.1.call-done = bf16[2048,2,1024]{2,0,1:T(8,128)(2,1)} async-done(((bf16[256,2,1024]{2,0,1:T(8,128)(2,1)}), bf16[2048,2,1024]{2,0,1:T(8,128)(2,1)}) %all-gather.5.cloned.1.call-update) | async-done | bytes 8388624 | tf_op jit(solution)/shard_map/all_gather | solution.py:147
  141.7 11.7 copy.140
  153.4 114.2 %all-gather.3.cloned.1.call-done = bf16[2048,2,1024]{2,0,1:T(8,128)(2,1)} async-done(((bf16[256,2,1024]{2,0,1:T(8,128)(2,1)}), bf16[2048,2,1024]{2,0,1:T(8,128)(2,1)}) %all-gather.3.cloned.1.call-update) | async-done | bytes 8388624 | tf_op jit(solution)/shard_map/all_gather | solution.py:146
  267.6 11.5 copy.139
  279.1 144.7 %while.28 = (s32[]{:T(128)}, f32[2,16,256]{2,1,0:T(8,128)S(1)}, f32[2,16,256]{2,1,0:T(8,128)S(1)}, f32[2,16,256,64]{2,3,1,0:T(8,128)}, s32[4]{0:T(128)S(1)}, /*i...) while((s32[]{:T(128)}, f32[2,16,256]{2,1,0:T(8,128)S(1)}, ...), condition=%wide.region_7.8_spmd.clone, body=%wide.region_4.0_spmd.clone.sunk | while | flops 1122149120 | bytes 70013144 | solution.py:156
  303.7 11.1 fusion.161
  339.4 11.7 fusion.161
  375.7 11.7 fusion.161
  412.0 11.7 fusion.161
  436.6 10.4 multiply_convert_fusion.1
  465.8 192.9 %while.29 = (s32[]{:T(128)}, f32[256,2,16,64]{0,3,2,1:T(8,128)}, bf16[4,512,2,2048]{1,3,2,0:T(8,128)(2,1)}, bf16[4,512,2,1024]{1,3,2,0:T(8,128)(2,1)}, s32[4]{0:...) while((s32[]{:T(128)}, f32[256,2,16,64]{0,3,2,1:T(8,128)}, ...), condition=%wide.region_12.13_spmd.clone, body=%wide.region_11.12_spmd.clone.sunk | while | flops 2739012352 | bytes 129093912 | solution.py:249
  483.7 10.6 fusion.174
  530.7 10.6 fusion.174
  579.3 10.6 fusion.174
  627.8 10.6 fusion.174
  658.7 21.6 %copy.148 = bf16[4,512,2,2048]{3,1,0,2:T(8,128)(2,1)} copy(bf16[4,512,2,2048]{1,3,2,0:T(8,128)(2,1)} %get-tuple-element.145) | data formatting | bytes 33554432 | tf_op jit(solution)/shard_map/convert_element_type | solution.py:260
  709.0 251.6 %reduce-scatter.30.cloned.1.call-done = bf16[256,2,2048]{2,0,1:T(8,128)(2,1)} async-done(((bf16[2048,2,2048]{2,0,1:T(8,128)(2,1)}), bf16[256,2,2048]{2,0,1:T(8,128)(2,1)}) %reduce-scatter.30.cloned.1.call-update) | async-done | bytes 2097168 | tf_op jit(solution)/shard_map/reduce_scatter | solution.py:259
  967.9 26.4 %reduce-scatter.38.cloned.1.call-done = bf16[256,1024]{1,0:T(8,128)(2,1)} async-done(((bf16[1024,1024]{1,0:T(8,128)(2,1)}), bf16[256,1024]{1,0:T(8,128)(2,1)}) %reduce-scatter.38.cloned.1.call-update) | async-done | bytes 524304 | tf_op jit(solution)/shard_map/reduce_scatter | solution.py:291
  996.4 55.2 %reduce-scatter.40.cloned.1.call-done = bf16[256,2816]{1,0:T(8,128)(2,1)} async-done(((bf16[1024,2816]{1,0:T(8,128)(2,1)}), bf16[256,2816]{1,0:T(8,128)(2,1)}) %reduce-scatter.40.cloned.1.call-update) | async-done | bytes 1441808 | tf_op jit(solution)/shard_map/reduce_scatter | solution.py:294
  1054.2 54.8 %reduce-scatter.42.cloned.1.call-done = bf16[256,2816]{1,0:T(8,128)(2,1)} async-done(((bf16[1024,2816]{1,0:T(8,128)(2,1)}), bf16[256,2816]{1,0:T(8,128)(2,1)}) %reduce-scatter.42.cloned.1.call-update) | async-done | bytes 1441808 | tf_op jit(solution)/shard_map/reduce_scatter | solution.py:297
  1111.7 54.8 %reduce-scatter.44.cloned.1.call-done = bf16[704,1024]{1,0:T(8,128)(2,1)} async-done(((bf16[2816,1024]{1,0:T(8,128)(2,1)}), bf16[704,1024]{1,0:T(8,128)(2,1)}) %reduce-scatter.44.cloned.1.call-update) | async-done | bytes 1441808 | tf_op jit(solution)/shard_map/reduce_scatter | solution.py:300
  1187.5 13.2 reduce-scatter.36.cloned.1.call-done
  1214.4 51.5 %reduce-scatter.52.cloned.1.call-done = bf16[128,256]{1,0:T(8,128)(2,1)} async-done(((bf16[1024,256]{1,0:T(8,128)(2,1)}), bf16[128,256]{1,0:T(8,128)(2,1)}) %reduce-scatter.52.cloned.1.call-update) | async-done | bytes 65552
  1267.6 66.0 %reduce-scatter.54.cloned.1.call-done = bf16[352,256]{1,0:T(8,128)(2,1)} async-done(((bf16[2816,256]{1,0:T(8,128)(2,1)}), bf16[352,256]{1,0:T(8,128)(2,1)}) %reduce-scatter.54.cloned.1.call-update) | async-done | bytes 180240
  1335.5 65.7 %reduce-scatter.56.cloned.1.call-done = bf16[352,256]{1,0:T(8,128)(2,1)} async-done(((bf16[2816,256]{1,0:T(8,128)(2,1)}), bf16[352,256]{1,0:T(8,128)(2,1)}) %reduce-scatter.56.cloned.1.call-update) | async-done | bytes 180240
  1403.2 65.4 %reduce-scatter.58.cloned.1.call-done = bf16[128,704]{1,0:T(8,128)(2,1)} async-done(((bf16[1024,704]{1,0:T(8,128)(2,1)}), bf16[128,704]{1,0:T(8,128)(2,1)}) %reduce-scatter.58.cloned.1.call-update) | async-done | bytes 180240
  1470.5 31.6 %reduce-scatter.34.cloned.1.call-done = bf16[256,1024]{1,0:T(8,128)(2,1)} async-done(((bf16[1024,1024]{1,0:T(8,128)(2,1)}), bf16[256,1024]{1,0:T(8,128)(2,1)}) %reduce-scatter.34.cloned.1.call-update) | async-done | bytes 524304 | tf_op jit(solution)/shard_map/reduce_scatter | solution.py:285
  1514.2 21.9 %reduce-scatter.32.cloned.1.call-done = bf16[256,1024]{1,0:T(8,128)(2,1)} async-done(((bf16[1024,1024]{1,0:T(8,128)(2,1)}), bf16[256,1024]{1,0:T(8,128)(2,1)}) %reduce-scatter.32.cloned.1.call-update) | async-done | bytes 524304 | tf_op jit(solution)/shard_map/reduce_scatter | solution.py:282
  1544.2 39.7 %all-reduce = (f32[1024]{0:T(1024)}, f32[1024]{0:T(1024)}, f32[]{:T(128)}, f32[]{:T(128)}) all-reduce(f32[1024]{0:T(1024)S(1)} %get-tuple-element.384, f32[1024]{0:T(1024)S(1)} %copy-done.32, f32[]{:T(128)} %fusion.47, f32[]{:T(128)} %get-tuple-element.459), channel_id=1, replica_groups=mesh['dp'=4,'blk'=8] {'dp','blk'}, use_global_device_ids=true, to_apply=%region_30.31 | all-reduce | flops 2050 | bytes 16400 | tf_op jit(solution)/shard_map/psum | solution.py:327
  1590.9 10.4 reduce-scatter.50.cloned.1.call-done
  1602.9 62.8 %reduce-scatter.48.cloned.1.call-done = bf16[128,256]{1,0:T(8,128)(2,1)} async-done(((bf16[1024,256]{1,0:T(8,128)(2,1)}), bf16[128,256]{1,0:T(8,128)(2,1)}) %reduce-scatter.48.cloned.1.call-update) | async-done | bytes 65552
  1667.3 62.6 %reduce-scatter.46.cloned.1.call-done = bf16[128,256]{1,0:T(8,128)(2,1)} async-done(((bf16[1024,256]{1,0:T(8,128)(2,1)}), bf16[128,256]{1,0:T(8,128)(2,1)}) %reduce-scatter.46.cloned.1.call-update) | async-done | bytes 65552
  (301 shorter events, 415.0 us)
Async XLA Ops:
  7.2 134.5 %all-gather.5.cloned.1.call-start = ((), (), s32[]{:S(2)}) async-start(), calls=%async_computation.16 | async-start | bytes 9437184 | tf_op jit(solution)/shard_map/all_gather | solution.py:147
  9.1 18.2 %copy-start.28 = (f32[256,2]{0,1:T(2,128)}, f32[256,2]{0,1:T(2,128)S(1)}, u32[]{:S(2)}) copy-start(f32[256,2]{0,1:T(2,128)S(1)} %add_rsqrt_fusion.1) | copy-start | bytes 6148
  13.9 253.7 %all-gather.3.cloned.1.call-start = ((), (), s32[]{:S(2)}) async-start(), calls=%async_computation.15 | async-start | bytes 9437184 | tf_op jit(solution)/shard_map/all_gather | solution.py:146
  31.8 928.8 %reduce-scatter.30.cloned.1.call-start = ((), (), s32[]{:S(2)}) async-start(), calls=%async_computation.17 | async-start | bytes 18874368 | tf_op jit(solution)/shard_map/reduce_scatter | solution.py:259
  426.4 10.2 slice-start.2
  427.8 29.2 %copy-start.3 = (f32[256,2,1024]{2,0,1:T(8,128)}, f32[256,2,1024]{2,0,1:T(8,128)S(1)}, u32[]{:S(2)}) copy-start(f32[256,2,1024]{2,0,1:T(8,128)S(1)} %get-tuple-element.470) | copy-start | bytes 6291460
  428.1 8.4 copy-start.15
  428.1 8.4 slice-start.3
  428.1 18.9 %slice-start = ((s8[5767168]{0:T(1024)(128)(4,1)}), s8[4194304]{0:T(1024)(128)(4,1)S(1)}, s32[]{:S(2)}) async-start(s8[5767168]{0:T(1024)(128)(4,1)} %bitcast.283), calls=%async_computation.32 | async-start | bytes 8388608
  436.6 10.4 slice-start.1
  447.0 6.0 copy-start.33
  494.2 9.4 copy-start.2
  541.3 9.4 copy-start.2
  589.9 9.4 copy-start.2
  638.4 9.4 copy-start.2
  680.4 313.9 %reduce-scatter.38.cloned.1.call-start = ((), (), s32[]{:S(2)}) async-start(), calls=%async_computation.21 | async-start | bytes 2621440 | tf_op jit(solution)/shard_map/reduce_scatter | solution.py:291
  685.8 365.8 %reduce-scatter.40.cloned.1.call-start = ((), (), s32[]{:S(2)}) async-start(), calls=%async_computation.22 | async-start | bytes 7208960 | tf_op jit(solution)/shard_map/reduce_scatter | solution.py:294
  693.9 415.1 %reduce-scatter.42.cloned.1.call-start = ((), (), s32[]{:S(2)}) async-start(), calls=%async_computation.23 | async-start | bytes 7208960 | tf_op jit(solution)/shard_map/reduce_scatter | solution.py:297
  700.8 465.7 %reduce-scatter.44.cloned.1.call-start = ((), (), s32[]{:S(2)}) async-start(), calls=%async_computation.24 | async-start | bytes 7208960 | tf_op jit(solution)/shard_map/reduce_scatter | solution.py:300
  709.0 255.9 %copy-start.7 = (bf16[256,2,1024]{2,1,0:T(2,128)(2,1)S(1)}, bf16[256,2,1024]{2,1,0:T(2,128)(2,1)}, u32[]{:S(2)}) copy-start(bf16[256,2,1024]{2,1,0:T(2,128)(2,1)} %param.17) | copy-start | bytes 3145732
  709.0 255.9 %copy-start.27 = (f32[1024]{0:T(1024)S(1)}, f32[1024]{0:T(1024)}, u32[]{:S(2)}) copy-start(f32[1024]{0:T(1024)} %param.27) | copy-start | bytes 12292
  709.0 255.9 %copy-start.29 = (f32[256,2]{0,1:T(2,128)S(1)}, f32[256,2]{0,1:T(2,128)}, u32[]{:S(2)}) copy-start(f32[256,2]{0,1:T(2,128)} %copy-done.28) | copy-start | bytes 6148
  709.0 491.7 %reduce-scatter.36.cloned.1.call-start = ((), (), s32[]{:S(2)}) async-start(), calls=%async_computation.20 | async-start | bytes 2621440 | tf_op jit(solution)/shard_map/reduce_scatter | solution.py:288
  967.8 298.1 %reduce-scatter.52.cloned.1.call-start = ((), (), s32[]{:S(2)}) async-start(), calls=%async_computation.28 | async-start | bytes 589824
  996.3 337.2 %reduce-scatter.54.cloned.1.call-start = ((), (), s32[]{:S(2)}) async-start(), calls=%async_computation.29 | async-start | bytes 1622016
  1054.2 347.0 %reduce-scatter.56.cloned.1.call-start = ((), (), s32[]{:S(2)}) async-start(), calls=%async_computation.30 | async-start | bytes 1622016
  1111.6 357.0 %reduce-scatter.58.cloned.1.call-start = ((), (), s32[]{:S(2)}) async-start(), calls=%async_computation.31 | async-start | bytes 1769472
  1169.1 333.0 %reduce-scatter.34.cloned.1.call-start = ((), (), s32[]{:S(2)}) async-start(), calls=%async_computation.19 | async-start | bytes 2621440 | tf_op jit(solution)/shard_map/reduce_scatter | solution.py:285
  1183.1 353.0 %reduce-scatter.32.cloned.1.call-start = ((), (), s32[]{:S(2)}) async-start(), calls=%async_computation.18 | async-start | bytes 2621440 | tf_op jit(solution)/shard_map/reduce_scatter | solution.py:282
  1187.4 413.8 %reduce-scatter.50.cloned.1.call-start = ((), (), s32[]{:S(2)}) async-start(), calls=%async_computation.27 | async-start | bytes 589824
  1202.7 463.0 %reduce-scatter.48.cloned.1.call-start = ((), (), s32[]{:S(2)}) async-start(), calls=%async_computation.26 | async-start | bytes 589824
  1504.1 225.8 %reduce-scatter.46.cloned.1.call-start = ((), (), s32[]{:S(2)}) async-start(), calls=%async_computation.25 | async-start | bytes 589824
  (29 other events, 77.4 us)
Sparse Core Ops, SparseCore 0:
  14.1 127.5 all-gather.4
  144.5 123.0 all-gather.2
  680.5 280.1 reduce-scatter.29
  963.8 30.4 reduce-scatter.37
  996.7 54.8 reduce-scatter.39
  1054.1 54.8 reduce-scatter.41
  1111.6 54.8 reduce-scatter.43
  1169.2 31.4 reduce-scatter.35
  1204.0 61.8 reduce-scatter.51
  1269.6 63.9 reduce-scatter.53
  1337.4 63.8 reduce-scatter.55
  1404.9 63.6 reduce-scatter.57
  1471.7 30.3 reduce-scatter.33
  1504.6 31.4 reduce-scatter.31
  1539.3 61.9 reduce-scatter.49
  1604.8 60.8 reduce-scatter.47
  1668.9 60.9 reduce-scatter.45
where the time goes:
time: 1750 us; the launch traced here: 1740 us
  waiting for transfers between devices  1110 us (63%)
  matrix products  317 us (18%)
  local copies, waits for them, and re-layouts  150 us (9%)
  other arithmetic  89.3 us (5%)
  blocking collectives  39.7 us (2%)
  between operations  18.2 us (1%)
    unnamed x24, waiting for transfers between devices  385 us
    reduce_scatter x1, waiting for transfers between devices, body(): lax.psum_scatter(terms.astype(jnp.bfloat16), 'blk', scatter_dimension=0,...  252 us
    all_gather x1, waiting for transfers between devices, body(): key_piece = lax.all_gather(keys_rot, 'blk', axis=0, tiled=True)  114 us
    all_gather x1, waiting for transfers between devices, body(): value_piece = lax.all_gather(mixed_low, 'blk', axis=0, tiled=True)  99.5 us
    unnamed x95, local copies, waits for them, and re-layouts  72 us
    reduce_scatter x1, waiting for transfers between devices, body(): lax.psum_scatter(weight_grads[4].astype(jnp.bfloat16), 'dp', scatter_dime...  55.2 us
    reduce_scatter x1, waiting for transfers between devices, body(): lax.psum_scatter(weight_grads[6].astype(jnp.bfloat16), 'dp', scatter_dime...  54.8 us
    reduce_scatter x1, waiting for transfers between devices, body(): lax.psum_scatter(weight_grads[5].astype(jnp.bfloat16), 'dp', scatter_dime...  54.8 us
  transfers between devices with their start and end apart: 17, of which 17 were waited for; matrix products, arithmetic and copies ran while one was open for 8% of the time, Pallas kernels for 0%

commit v1 on v0

--- a/solution.py
+++ b/solution.py
@@ -6,6 +6,12 @@
 HEADS = 16
 HEAD_DIM = 64
 epsilon = 1e-06
+
+
+def shape_pools(incoming_x, shard_in):
+    spare = jnp.concatenate([incoming_x, shard_in], axis=1)
+    v1 = lax.all_gather(spare, "blk", axis=0, tiled=True)
+    return jnp.split(v1, [incoming_x.shape[1]], axis=1)
 
 
 def documents(doc_lengths, row_length):
@@ -143,8 +149,7 @@
         jnp.zeros((seq_count, HEADS, local_len, HEAD_DIM), jnp.float32),
     )
     running = start_state
-    key_piece = lax.all_gather(keys_rot, "blk", axis=0, tiled=True)
-    value_piece = lax.all_gather(mixed_low, "blk", axis=0, tiled=True)
+    key_piece, value_piece = shape_pools(keys_rot, mixed_low)
     n_keys = key_piece.shape[0]
     step_rows = min(512, n_keys)
     n_steps = n_keys // step_rows

time: 1750 us -> 1850 us (1.057)
  local copies, waits for them, and re-layouts: 150 us -> 206 us
  matrix products: 317 us -> 340 us
    dynamic_slice x16 -> x32, local copies, waits for them, and re-layouts: 35.2 us -> 105 us  [body(): lax.scan(inner_step, running, (key_piece.reshape(n_steps, step_rows, seq_...]
    unnamed x95 -> x89, local copies, waits for them, and re-layouts: 72 us -> 49.2 us
    all_gather x2 -> x3, waiting for transfers between devices: 214 us -> 221 us  [the longest x1 218 us: shape_pools(): v1 = lax.all_gather(spare, 'blk', axis=0, tiled=True)]
    unnamed x24 -> x25, waiting for transfers between devices: 385 us -> 386 us
  transfers between devices with their start and end apart: 17 -> 18, of which waited for: 17 -> 17; matrix products, arithmetic and copies ran while one was open for 8% -> 19% of each run, Pallas kernels for 0% -> 0%
where the time goes in v1:
time: 1850 us; the launch traced here: 1840 us
  waiting for transfers between devices  1120 us (61%)
  matrix products  340 us (18%)
  local copies, waits for them, and re-layouts  206 us (11%)
  other arithmetic  96.8 us (5%)
  blocking collectives  39.7 us (2%)
  between operations  18.6 us (1%)
    unnamed x25, waiting for transfers between devices  386 us
    reduce_scatter x1, waiting for transfers between devices, body(): lax.psum_scatter(terms.astype(jnp.bfloat16), 'blk', scatter_dimension=0,...  252 us
    all_gather x1, waiting for transfers between devices, shape_pools(): v1 = lax.all_gather(spare, 'blk', axis=0, tiled=True)  218 us
    dynamic_slice x32, local copies, waits for them, and re-layouts, body(): lax.scan(inner_step, running, (key_piece.reshape(n_steps, step_rows, seq_...  105 us
    reduce_scatter x1, waiting for transfers between devices, body(): lax.psum_scatter(weight_grads[4].astype(jnp.bfloat16), 'dp', scatter_dime...  55.2 us
    reduce_scatter x1, waiting for transfers between devices, body(): lax.psum_scatter(weight_grads[5].astype(jnp.bfloat16), 'dp', scatter_dime...  55 us
    reduce_scatter x1, waiting for transfers between devices, body(): lax.psum_scatter(weight_grads[6].astype(jnp.bfloat16), 'dp', scatter_dime...  54.8 us
    unnamed x89, local copies, waits for them, and re-layouts  49.2 us
  transfers between devices with their start and end apart: 18, of which 17 were waited for; matrix products, arithmetic and copies ran while one was open for 19% of the time, Pallas kernels for 0%

profile of v1, /device:TPU:0, one launch (start us, length us, event | category | flops | bytes accessed | tf_op | source)
XLA Modules:
  0.0 1835.4 jit_solution(2501318408022098649)
XLA Ops:
  55.0 217.7 %all-gather.4.cloned.1.call-done = bf16[2048,4,1024]{2,0,1:T(8,128)(2,1)} async-done(((bf16[256,4,1024]{2,0,1:T(8,128)(2,1)}), bf16[2048,4,1024]{2,0,1:T(8,128)(2,1)}) %all-gather.4.cloned.1.call-update) | async-done | bytes 16777232 | tf_op jit(solution)/shard_map/all_gather | solution.py:13
  272.7 12.6 fusion.101
  285.2 193.7 %while.28 = (s32[]{:T(128)}, f32[2,16,256]{2,1,0:T(8,128)S(1)}, f32[2,16,256]{2,1,0:T(8,128)S(1)}, f32[2,16,256,64]{2,3,1,0:T(8,128)}, s32[4]{0:T(128)S(1)}, /*i...) while((s32[]{:T(128)}, f32[2,16,256]{2,1,0:T(8,128)S(1)}, ...), condition=%wide.region_7.8_spmd.clone, body=%wide.region_4.0_spmd.clone.sunk | while | flops 1122149120 | bytes 78401752 | solution.py:161
  321.5 12.1 fusion.162
  350.6 10.1 fusion.159
  370.0 12.0 fusion.162
  398.9 10.9 fusion.159
  419.1 11.8 fusion.162
  467.1 11.7 fusion.162
  491.8 10.2 multiply_convert_fusion.1
  523.9 229.1 %while.29 = (s32[]{:T(128)}, f32[256,2,16,64]{0,3,2,1:T(8,128)}, bf16[4,512,2,2048]{1,3,2,0:T(8,128)(2,1)}, bf16[4,512,2,1024]{3,1,0,2:T(8,128)(2,1)}, s32[4]{0:...) while((s32[]{:T(128)}, f32[256,2,16,64]{0,3,2,1:T(8,128)}, ...), condition=%wide.region_12.13_spmd.clone, body=%wide.region_11.12_spmd.clone.sunk | while | flops 2739012352 | bytes 129093896 | solution.py:254
  550.7 10.6 fusion.175
  606.7 10.6 fusion.175
  664.2 10.6 fusion.175
  721.7 10.6 fusion.175
  752.9 21.7 %copy.153 = bf16[4,512,2,2048]{3,1,0,2:T(8,128)(2,1)} copy(bf16[4,512,2,2048]{1,3,2,0:T(8,128)(2,1)} %get-tuple-element.145) | data formatting | bytes 33554432 | tf_op jit(solution)/shard_map/convert_element_type | solution.py:265
  803.4 251.6 %reduce-scatter.30.cloned.1.call-done = bf16[256,2,2048]{2,0,1:T(8,128)(2,1)} async-done(((bf16[2048,2,2048]{2,0,1:T(8,128)(2,1)}), bf16[256,2,2048]{2,0,1:T(8,128)(2,1)}) %reduce-scatter.30.cloned.1.call-update) | async-done | bytes 2097168 | tf_op jit(solution)/shard_map/reduce_scatter | solution.py:264
  1062.1 26.5 %reduce-scatter.38.cloned.1.call-done = bf16[256,1024]{1,0:T(8,128)(2,1)} async-done(((bf16[1024,1024]{1,0:T(8,128)(2,1)}), bf16[256,1024]{1,0:T(8,128)(2,1)}) %reduce-scatter.38.cloned.1.call-update) | async-done | bytes 524304 | tf_op jit(solution)/shard_map/reduce_scatter | solution.py:296
  1090.7 55.2 %reduce-scatter.40.cloned.1.call-done = bf16[256,2816]{1,0:T(8,128)(2,1)} async-done(((bf16[1024,2816]{1,0:T(8,128)(2,1)}), bf16[256,2816]{1,0:T(8,128)(2,1)}) %reduce-scatter.40.cloned.1.call-update) | async-done | bytes 1441808 | tf_op jit(solution)/shard_map/reduce_scatter | solution.py:299
  1148.5 55.0 %reduce-scatter.42.cloned.1.call-done = bf16[256,2816]{1,0:T(8,128)(2,1)} async-done(((bf16[1024,2816]{1,0:T(8,128)(2,1)}), bf16[256,2816]{1,0:T(8,128)(2,1)}) %reduce-scatter.42.cloned.1.call-update) | async-done | bytes 1441808 | tf_op jit(solution)/shard_map/reduce_scatter | solution.py:302
  1206.1 54.8 %reduce-scatter.44.cloned.1.call-done = bf16[704,1024]{1,0:T(8,128)(2,1)} async-done(((bf16[2816,1024]{1,0:T(8,128)(2,1)}), bf16[704,1024]{1,0:T(8,128)(2,1)}) %reduce-scatter.44.cloned.1.call-update) | async-done | bytes 1441808 | tf_op jit(solution)/shard_map/reduce_scatter | solution.py:305
  1281.8 13.3 reduce-scatter.36.cloned.1.call-done
  1308.9 51.3 %reduce-scatter.52.cloned.1.call-done = bf16[128,256]{1,0:T(8,128)(2,1)} async-done(((bf16[1024,256]{1,0:T(8,128)(2,1)}), bf16[128,256]{1,0:T(8,128)(2,1)}) %reduce-scatter.52.cloned.1.call-update) | async-done | bytes 65552
  1361.9 66.0 %reduce-scatter.54.cloned.1.call-done = bf16[352,256]{1,0:T(8,128)(2,1)} async-done(((bf16[2816,256]{1,0:T(8,128)(2,1)}), bf16[352,256]{1,0:T(8,128)(2,1)}) %reduce-scatter.54.cloned.1.call-update) | async-done | bytes 180240
  1429.8 65.8 %reduce-scatter.56.cloned.1.call-done = bf16[352,256]{1,0:T(8,128)(2,1)} async-done(((bf16[2816,256]{1,0:T(8,128)(2,1)}), bf16[352,256]{1,0:T(8,128)(2,1)}) %reduce-scatter.56.cloned.1.call-update) | async-done | bytes 180240
  1497.6 65.7 %reduce-scatter.58.cloned.1.call-done = bf16[128,704]{1,0:T(8,128)(2,1)} async-done(((bf16[1024,704]{1,0:T(8,128)(2,1)}), bf16[128,704]{1,0:T(8,128)(2,1)}) %reduce-scatter.58.cloned.1.call-update) | async-done | bytes 180240
  1565.2 31.5 %reduce-scatter.34.cloned.1.call-done = bf16[256,1024]{1,0:T(8,128)(2,1)} async-done(((bf16[1024,1024]{1,0:T(8,128)(2,1)}), bf16[256,1024]{1,0:T(8,128)(2,1)}) %reduce-scatter.34.cloned.1.call-update) | async-done | bytes 524304 | tf_op jit(solution)/shard_map/reduce_scatter | solution.py:290
  1609.0 21.6 %reduce-scatter.32.cloned.1.call-done = bf16[256,1024]{1,0:T(8,128)(2,1)} async-done(((bf16[1024,1024]{1,0:T(8,128)(2,1)}), bf16[256,1024]{1,0:T(8,128)(2,1)}) %reduce-scatter.32.cloned.1.call-update) | async-done | bytes 524304 | tf_op jit(solution)/shard_map/reduce_scatter | solution.py:287
  1638.7 39.7 %all-reduce = (f32[1024]{0:T(1024)}, f32[1024]{0:T(1024)}, f32[]{:T(128)}, f32[]{:T(128)}) all-reduce(f32[1024]{0:T(1024)S(1)} %get-tuple-element.384, f32[1024]{0:T(1024)S(1)} %copy-done.29, f32[]{:T(128)} %fusion.47, f32[]{:T(128)} %get-tuple-element.461), channel_id=1, replica_groups=mesh['dp'=4,'blk'=8] {'dp','blk'}, use_global_device_ids=true, to_apply=%region_30.31 | all-reduce | flops 2050 | bytes 16400 | tf_op jit(solution)/shard_map/psum | solution.py:332
  1685.4 10.4 reduce-scatter.50.cloned.1.call-done
  1697.5 62.9 %reduce-scatter.48.cloned.1.call-done = bf16[128,256]{1,0:T(8,128)(2,1)} async-done(((bf16[1024,256]{1,0:T(8,128)(2,1)}), bf16[128,256]{1,0:T(8,128)(2,1)}) %reduce-scatter.48.cloned.1.call-update) | async-done | bytes 65552
  1762.0 62.5 %reduce-scatter.46.cloned.1.call-done = bf16[128,256]{1,0:T(8,128)(2,1)} async-done(((bf16[1024,256]{1,0:T(8,128)(2,1)}), bf16[128,256]{1,0:T(8,128)(2,1)}) %reduce-scatter.46.cloned.1.call-update) | async-done | bytes 65552
  (308 shorter events, 493.2 us)
Async XLA Ops:
  7.2 27.5 %copy-start = (bf16[1024,1024]{1,0:T(8,128)(2,1)S(1)}, bf16[1024,1024]{1,0:T(8,128)(2,1)}, u32[]{:S(2)}) copy-start(bf16[1024,1024]{1,0:T(8,128)(2,1)} %param.22) | copy-start | bytes 6291460
  7.2 265.5 %all-gather.4.cloned.1.call-start = ((), (), s32[]{:S(2)}) async-start(), calls=%async_computation.15 | async-start | bytes 18874368 | tf_op jit(solution)/shard_map/all_gather | solution.py:13
  9.8 24.9 %copy-start.26 = (f32[256,2]{0,1:T(2,128)}, f32[256,2]{0,1:T(2,128)S(1)}, u32[]{:S(2)}) copy-start(f32[256,2]{0,1:T(2,128)S(1)} %add_rsqrt_fusion.1) | copy-start | bytes 6148
  42.2 478.7 %all-gather.8.cloned.1.call-start = ((), (), s32[]{:S(2)}) async-start(), calls=%async_computation.17 | async-start | bytes 9437184 | tf_op jit(solution)/shard_map/all_gather | solution.py:206
  43.0 480.9 %all-gather.6.cloned.1.call-start = ((), (), s32[]{:S(2)}) async-start(), calls=%async_computation.16 | async-start | bytes 9437184 | tf_op jit(solution)/shard_map/all_gather | solution.py:205
  43.7 1011.2 %reduce-scatter.30.cloned.1.call-start = ((), (), s32[]{:S(2)}) async-start(), calls=%async_computation.18 | async-start | bytes 18874368 | tf_op jit(solution)/shard_map/reduce_scatter | solution.py:264
  481.5 10.3 slice-start.2
  482.9 29.1 %copy-start.2 = (f32[256,2,1024]{2,0,1:T(8,128)}, f32[256,2,1024]{2,0,1:T(8,128)S(1)}, u32[]{:S(2)}) copy-start(f32[256,2,1024]{2,0,1:T(8,128)S(1)} %get-tuple-element.472) | copy-start | bytes 6291460
  483.2 8.5 copy-start.14
  483.2 18.8 %slice-start = ((s8[5767168]{0:T(1024)(128)(4,1)}), s8[4194304]{0:T(1024)(128)(4,1)S(1)}, s32[]{:S(2)}) async-start(s8[5767168]{0:T(1024)(128)(4,1)} %bitcast.287), calls=%async_computation.33 | async-start | bytes 8388608
  491.8 10.2 slice-start.1
  561.4 9.4 copy-start.1
  617.3 9.4 copy-start.1
  674.8 9.4 copy-start.1
  732.3 9.4 copy-start.1
  774.7 313.9 %reduce-scatter.38.cloned.1.call-start = ((), (), s32[]{:S(2)}) async-start(), calls=%async_computation.22 | async-start | bytes 2621440 | tf_op jit(solution)/shard_map/reduce_scatter | solution.py:296
  780.1 365.8 %reduce-scatter.40.cloned.1.call-start = ((), (), s32[]{:S(2)}) async-start(), calls=%async_computation.23 | async-start | bytes 7208960 | tf_op jit(solution)/shard_map/reduce_scatter | solution.py:299
  788.2 415.3 %reduce-scatter.42.cloned.1.call-start = ((), (), s32[]{:S(2)}) async-start(), calls=%async_computation.24 | async-start | bytes 7208960 | tf_op jit(solution)/shard_map/reduce_scatter | solution.py:302
  795.1 465.8 %reduce-scatter.44.cloned.1.call-start = ((), (), s32[]{:S(2)}) async-start(), calls=%async_computation.25 | async-start | bytes 7208960 | tf_op jit(solution)/shard_map/reduce_scatter | solution.py:305
  803.3 255.8 %copy-start.6 = (bf16[256,2,1024]{2,1,0:T(2,128)(2,1)S(1)}, bf16[256,2,1024]{2,1,0:T(2,128)(2,1)}, u32[]{:S(2)}) copy-start(bf16[256,2,1024]{2,1,0:T(2,128)(2,1)} %param.17) | copy-start | bytes 3145732
  803.3 255.8 %copy-start.25 = (f32[1024]{0:T(1024)S(1)}, f32[1024]{0:T(1024)}, u32[]{:S(2)}) copy-start(f32[1024]{0:T(1024)} %param.27) | copy-start | bytes 12292
  803.3 255.8 %copy-start.27 = (f32[256,2]{0,1:T(2,128)S(1)}, f32[256,2]{0,1:T(2,128)}, u32[]{:S(2)}) copy-start(f32[256,2]{0,1:T(2,128)} %copy-done.26) | copy-start | bytes 6148
  803.3 491.7 %reduce-scatter.36.cloned.1.call-start = ((), (), s32[]{:S(2)}) async-start(), calls=%async_computation.21 | async-start | bytes 2621440 | tf_op jit(solution)/shard_map/reduce_scatter | solution.py:293
  1062.1 298.2 %reduce-scatter.52.cloned.1.call-start = ((), (), s32[]{:S(2)}) async-start(), calls=%async_computation.29 | async-start | bytes 589824
  1090.7 337.2 %reduce-scatter.54.cloned.1.call-start = ((), (), s32[]{:S(2)}) async-start(), calls=%async_computation.30 | async-start | bytes 1622016
  1148.4 347.2 %reduce-scatter.56.cloned.1.call-start = ((), (), s32[]{:S(2)}) async-start(), calls=%async_computation.31 | async-start | bytes 1622016
  1206.0 357.3 %reduce-scatter.58.cloned.1.call-start = ((), (), s32[]{:S(2)}) async-start(), calls=%async_computation.32 | async-start | bytes 1769472
  1263.5 333.1 %reduce-scatter.34.cloned.1.call-start = ((), (), s32[]{:S(2)}) async-start(), calls=%async_computation.20 | async-start | bytes 2621440 | tf_op jit(solution)/shard_map/reduce_scatter | solution.py:290
  1277.6 353.0 %reduce-scatter.32.cloned.1.call-start = ((), (), s32[]{:S(2)}) async-start(), calls=%async_computation.19 | async-start | bytes 2621440 | tf_op jit(solution)/shard_map/reduce_scatter | solution.py:287
  1281.7 414.1 %reduce-scatter.50.cloned.1.call-start = ((), (), s32[]{:S(2)}) async-start(), calls=%async_computation.28 | async-start | bytes 589824
  1297.2 463.2 %reduce-scatter.48.cloned.1.call-start = ((), (), s32[]{:S(2)}) async-start(), calls=%async_computation.27 | async-start | bytes 589824
  1598.7 225.8 %reduce-scatter.46.cloned.1.call-start = ((), (), s32[]{:S(2)}) async-start(), calls=%async_computation.26 | async-start | bytes 589824
  (24 other events, 74.6 us)
Sparse Core Ops, SparseCore 0:
  42.3 230.2 all-gather.3
  275.4 123.0 all-gather.7
  400.7 123.0 all-gather.5
  774.8 280.0 reduce-scatter.29
  1058.0 30.4 reduce-scatter.37
  1091.0 54.8 reduce-scatter.39
  1148.6 54.8 reduce-scatter.41
  1206.0 54.8 reduce-scatter.43
  1263.6 31.4 reduce-scatter.35
  1298.3 61.9 reduce-scatter.51
  1364.0 63.8 reduce-scatter.53
  1431.5 64.0 reduce-scatter.55
  1499.5 63.8 reduce-scatter.57
  1566.3 30.3 reduce-scatter.33
  1599.2 31.3 reduce-scatter.31
  1633.8 61.9 reduce-scatter.49
  1699.4 60.9 reduce-scatter.47
  1763.6 60.8 reduce-scatter.45
